TPU v7x, 128 devices: a whole 4x4x4 slice. The times are simulated.
128 devices in a mesh: dom: 128 (over y, x, z, core).
Axes of the slice: x: 4, y: 4, z: 4, core: 2. Of those that a mesh axis runs over, the one named last changes fastest.
Arguments:
- coefficients: float32 [56, 9, 32768], P(None, None, 'dom'), may hold values from -6 to 6
- star_matrices: float32 [3, 9, 9, 32768], P(None, None, None, 'dom'), may hold values from -3 to 3
- own_flux: float32 [9, 9, 4, 32768], P(None, None, None, 'dom'), may hold values from -2 to 2
- neighbour_flux: float32 [9, 9, 4, 32768], P(None, None, None, 'dom'), may hold values from -2 to 2
- stiffness: float32 [3, 56, 56], replicated, may hold values from -0.75 to 0.75
- projection: float32 [4, 21, 56], replicated, may hold values from -0.75 to 0.75
- rotation: float32 [3, 21, 21], replicated, may hold values from -1.25 to 1.25
- fault_minus: float32 [9, 9, 16384], P(None, None, 'dom'), may hold values from -2 to 2
- fault_plus: float32 [9, 9, 16384], P(None, None, 'dom'), may hold values from -2 to 2
- slip_compliance: float32 [16384], P('dom'), may hold values from 0.1 to 10
- neighbour_slot: int32 [4, 32768], P(None, 'dom'), may hold values from 0 to 767
- neighbour_code: int32 [4, 32768], P(None, 'dom'), may hold values from 0 to 11, as said below
- halo_send: int32 [4, 16384], P(None, 'dom'), may hold values from 0 to 1023, as said below
- fault_table: int32 [3, 16384], P(None, 'dom'), may hold values from -1 to 1023, as said below
Outputs:
- next_coefficients: float32 [56, 9, 32768], P(None, None, 'dom')
Inputs may be any that keep to these rules, and one draw needn't show every extreme that they name: `neighbour_code`: 3 j + h; for a face whose slot is 256 or more, j equals the matching halo_send entry // 256. `halo_send`: row o, slot s of a device: j * 256 + e, face j of its element e, whose data go to the device at index plus shift[o] (shift = 1, 2, -1, -2, cyclic). `fault_table`: exactly a quarter of the devices own fault faces, drawn from the seed; a device's columns c * 1 to c + 1 - 1 hold its faces for owner c, all filled if c owns and -1, -1, 0 if not; the faces named on one device all differ.
All inputs are finite; a program needn't handle non-finite values.
Results may differ from a plain program's by a relative error of at most 0.0003.
Values sent between devices are 32-bit elements; how exact they have to be, the bound alone decides.
No kernel may reach another device: no remote copies, remote signals or barrier semaphores. Data moves between devices by JAX's collectives and lax.ppermute only.
A program may use at most 192 MiB of HBM per device.

v0:
```python
import functools
import jax
import jax.numpy as jnp
from jax import lax
from jax.experimental import pallas as pl
from jax.experimental.pallas import tpu as pltpu
from jax.sharding import PartitionSpec as P


ORDER = 6
SHIFTS = (1, 2, -1, -2)
F32 = jnp.float32
BF16 = jnp.bfloat16

NB, NQ, NM, NF, NE, NS = 56, 9, 21, 4, 256, 128
MP = 24
BP = 64
RT = NQ * MP
ETA_ROW = 176
PLUS_ROW = 88
GROUPS = ((0, 16), (16, 16), (32, 24))
QL = NQ * 128


def split(x):
    hi = x.astype(BF16)
    lo = (x - hi.astype(F32)).astype(BF16)
    return hi, lo


def dot(a, b):
    return jnp.dot(a, b, preferred_element_type=F32)


def dot_t(a, b):
    return lax.dot_general(a, b, (((1,), (1,)), ((), ())), preferred_element_type=F32)


def put_weights(ref, rows, w, width):
    hi, lo = split(w)
    k = w.shape[1]
    ref[rows, 0:k] = hi
    ref[rows, width : width + k] = lo
    ref[rows, 2 * width : 2 * width + k] = hi


def put_split(ref, q, row, count, x):
    hi, lo = split(x)
    ref[row : row + count, q * 128 : (q + 1) * 128] = hi
    ref[BP + row : BP + row + count, q * 128 : (q + 1) * 128] = lo


def doubled(ref):
    return jnp.concatenate([ref[0:BP], ref[0:BP], ref[BP : 2 * BP]], 0)


def mix_star(t_ref, star_ref, row, count, lanes):
    acc = [None] * NQ
    for p in range(NQ):
        for i in range(3):
            t = t_ref[i * NB + row : i * NB + row + count, p * 128 : (p + 1) * 128]
            for q in range(NQ):
                s = jnp.broadcast_to(star_ref[p, q, i : i + 1, lanes], (count, 128))
                acc[q] = t * s if acc[q] is None else acc[q] + t * s
    return acc


def mix_flux(src_ref, flux_ref, face, lanes):
    acc = [None] * NQ
    for p in range(NQ):
        t = src_ref[face, p * MP : (p + 1) * MP, lanes]
        for q in range(NQ):
            s = jnp.broadcast_to(flux_ref[p, q, face : face + 1, lanes], (MP, 128))
            acc[q] = t * s if acc[q] is None else acc[q] + t * s
    return acc


def one_by_one(count, step):
    def body(i, c):
        for j in range(count):
            pl.when(i == j)(functools.partial(step, j, i))
        return c

    lax.fori_loop(0, count, body, 0)


HALVES = (slice(0, 128), slice(128, 256))


def put_iota(ref):
    ref[...] = lax.broadcasted_iota(jnp.int32, ref.shape, 0).astype(F32).astype(BF16)


def put_one_hot(ref, ids, iota_ref, faces):
    one, zero = jnp.ones((), BF16), jnp.zeros((), BF16)
    for s in range(faces):
        at = ids - s * NE
        at = jnp.where((at >= 0) & (at < NE), at, -1).astype(F32).astype(BF16)
        ref[s * NE : (s + 1) * NE, :] = jnp.where(
            iota_ref[...] == jnp.broadcast_to(at, (NE, NE)), one, zero
        )


def named(names, refs):
    return dict(zip(names, refs))


class Copies:
    def __init__(self, sems):
        self.sems, self.count, self.open = sems, 0, {}

    def made(self, a, b, at, number):
        if at is not None:
            a, b = a.at[at], b.at[at]
        return pltpu.make_async_copy(a, b, self.sems.at[number])

    def reserve(self, names, a, b):
        first = self.count
        for i, name in enumerate(names):
            self.open[name] = (a, b, i, first + i)
        self.count += len(names)
        return lambda i: self.made(a, b, i, first + i).start()

    def start(self, name, a, b, at=None):
        self.open[name] = (a, b, at, self.count)
        self.count += 1
        self.made(*self.open[name]).start()

    def wait(self, *names):
        for name in names:
            self.made(*self.open.pop(name)).wait()

    def finish(self):
        for one in self.open.values():
            self.made(*one).wait()


FIRST_IN = ("stiff", "proj", "coef", "star", "minus", "plus", "eta", "send")
FIRST_OUT = ("packed", "xs0", "xs1", "tr", "th", "tl", "p0", "p1", "p2", "p3")
FIRST_TMP = ("t0", "t1", "w", "int", "pw", "hot", "hot2", "iota", "scr")
FIRST_COPIES = 8 + 6 + 4 + 4


def first_kernel(*refs):
    ni, no = len(FIRST_IN), len(FIRST_OUT)
    hbm = named(FIRST_IN + FIRST_OUT, refs[: ni + no])
    v = named(FIRST_IN + FIRST_OUT, refs[ni + no : 2 * (ni + no)])
    t = named(FIRST_TMP, refs[2 * (ni + no) : -1])
    copies = Copies(refs[-1])
    for name in FIRST_IN:
        copies.start(name, hbm[name], v[name])

    def send(name, *at):
        copies.start((name, at), v[name], hbm[name], *at)

    xs, ts, star_ref, int_ref = (v["xs0"], v["xs1"]), (t["t0"], t["t1"]), v["star"], t["int"]
    w_ref, pw_ref, iota_ref, scr = t["w"], t["pw"], t["iota"], t["scr"]
    w_ref[...] = jnp.zeros_like(w_ref)
    pw_ref[...] = jnp.zeros_like(pw_ref)
    scr[...] = jnp.zeros_like(scr)
    put_iota(iota_ref)
    for x in xs:
        for part in range(2):
            x[part * BP + NB : (part + 1) * BP, :] = jnp.zeros((BP - NB, QL), BF16)
    copies.wait("stiff", "proj")
    for i in range(3):
        put_weights(w_ref, slice(i * NB, (i + 1) * NB), v["stiff"][i], BP)
    for f in range(NF):
        put_weights(pw_ref, slice(f * MP, f * MP + NM), v["proj"][:, f, :], BP)
    copies.wait("coef", "star")

    def start(q, c):
        for h in range(2):
            at = pl.ds(pl.multiple_of(q * 128, 128), 128)
            x = v["coef"][q, :, HALVES[h]]
            int_ref[q, :, HALVES[h]] = x
            hi, lo = split(x)
            xs[h][0:NB, at] = hi
            xs[h][BP : BP + NB, at] = lo
        return c

    lax.fori_loop(0, NQ, start, 0)
    copies.wait("minus", "plus", "eta")
    for p in range(NQ):
        scr[p * NQ : (p + 1) * NQ, :] = v["minus"][p]
        scr[PLUS_ROW + p * NQ : PLUS_ROW + (p + 1) * NQ, :] = v["plus"][p]
    scr[ETA_ROW : ETA_ROW + 1, :] = v["eta"][...]
    v["packed"][:, 0, :] = scr[0:128, :].T
    v["packed"][:, 1, :] = scr[128:256, :].T
    send("packed")
    ts[0][...] = dot(w_ref[...], doubled(xs[0]))

    def mixed(h, factor):
        for row, count in GROUPS:
            acc = mix_star(ts[h], star_ref, row, count, HALVES[h])
            for q in range(NQ):
                put_split(xs[h], q, row, count, acc[q])
                int_ref[q, row : row + count, HALVES[h]] += factor * acc[q]

    def stage(k, factor):
        factor = factor / (k + 2).astype(F32)

        @pl.when(k >= 0)
        def _():
            ts[1][...] = dot(w_ref[...], doubled(xs[1]))
            mixed(0, factor)

        @pl.when(k < ORDER)
        def _():
            ts[0][...] = dot(w_ref[...], doubled(xs[0]))
            mixed(1, factor)

        return factor

    lax.fori_loop(0, ORDER - 1, stage, jnp.float32(1.0))

    def finish(q, c):
        for h in range(2):
            at = pl.ds(pl.multiple_of(q * 128, 128), 128)
            hi, lo = split(int_ref[q, :, HALVES[h]])
            xs[h][0:NB, at] = hi
            xs[h][BP : BP + NB, at] = lo
        return c

    lax.fori_loop(0, NQ, finish, 0)
    send("xs0")
    send("xs1")
    th_ref, tl_ref, tr_ref = v["th"], v["tl"], v["tr"]
    for h in range(2):
        tall = ts[h]
        tall[0 : NF * MP, :] = dot(pw_ref[...], doubled(xs[h]))
    for f in range(NF):
        for h in range(2):
            x = jnp.concatenate(
                [ts[h][f * MP : (f + 1) * MP, q * 128 : (q + 1) * 128] for q in range(NQ)], 0
            )
            tr_ref[f, :, HALVES[h]] = x
            hi, lo = split(x)
            at = slice(f * NE + h * 128, f * NE + (h + 1) * 128)
            th_ref[:, at] = hi
            tl_ref[:, at] = lo

    def picked(hot):
        return dot(th_ref[...], hot[...]) + dot(tl_ref[...], hot[...])

    copies.wait("send")
    for name in ("th", "tl", "tr"):
        send(name)
    for o in range(0, NF, 2):
        send_ref = v["send"]
        ids = jnp.concatenate([send_ref[o : o + 1, :], send_ref[o + 1 : o + 2, :]], 1)
        hot = t["hot"] if o == 0 else t["hot2"]
        put_one_hot(hot, ids, iota_ref, NF)
        got = picked(hot)
        v[f"p{o}"][...] = got[:, :NS]
        v[f"p{o + 1}"][...] = got[:, NS:]
        send(f"p{o}")
        send(f"p{o + 1}")
    copies.finish()


NEAR_IN = ("stiff", "proj", "xs0", "xs1", "star", "coef", "table", "slot", "code", "rot", "th", "tl", "tr", "own")
NEAR_OUT = ("part", "g", "pair", "wf", "pt", "rtw", "idr")
NEAR_TMP = ("t0", "t1", "wv", "hot", "iota", "st", "fhot", "raw", "free", "ids", "rw")
NEAR_COPIES = 14 + 6 + 4


def near_kernel(*refs):
    ni, no = len(NEAR_IN), len(NEAR_OUT)
    hbm = named(NEAR_IN + NEAR_OUT, refs[: ni + no])
    v = named(NEAR_IN + NEAR_OUT, refs[ni + no : 2 * (ni + no)])
    t = named(NEAR_TMP, refs[2 * (ni + no) : -1])
    copies = Copies(refs[-1])
    for name in NEAR_IN:
        copies.start(name, hbm[name], v[name])

    def send(name, *at):
        copies.start((name, at), v[name], hbm[name], *at)

    xs, ts, star_ref = (v["xs0"], v["xs1"]), (t["t0"], t["t1"]), v["star"]
    wv_ref, iota_ref, pt_ref, part_ref = t["wv"], t["iota"], v["pt"], v["part"]
    th_ref, tl_ref, tr_ref, hot_ref = v["th"], v["tl"], v["tr"], t["hot"]
    wv_ref[...] = jnp.zeros_like(wv_ref)
    pt_ref[...] = jnp.zeros_like(pt_ref)
    put_iota(iota_ref)
    copies.wait("stiff", "proj")
    for i in range(3):
        put_weights(wv_ref, slice(i * NB, (i + 1) * NB), v["stiff"][i].T, BP)
    for f in range(NF):
        hi, lo = split(v["proj"][:, f, :].T)
        pt_ref[:, f * MP : f * MP + NM] = hi
        pt_ref[:, 96 + f * MP : 96 + f * MP + NM] = lo
        pt_ref[:, 192 + f * MP : 192 + f * MP + NM] = hi
    send("pt")

    def volume(h, i):
        if h == 0:
            ts[1][...] = dot(wv_ref[...], doubled(xs[1]))
        for row, count in GROUPS:
            acc = mix_star(ts[h], star_ref, row, count, HALVES[h])
            for q in range(NQ):
                x = v["coef"][q, row : row + count, HALVES[h]]
                part_ref[q, row : row + count, HALVES[h]] = x + acc[q]

    copies.wait("xs0", "xs1")
    ts[0][...] = dot(wv_ref[...], doubled(xs[0]))
    copies.wait("star", "coef")
    one_by_one(2, volume)

    def picked(hot):
        return dot(th_ref[...], hot[...]) + dot(tl_ref[...], hot[...])

    copies.wait("table", "slot", "code", "th", "tl", "tr", "own")
    table = v["table"][...]
    active = table[0:1] >= 0
    ids = jnp.concatenate([jnp.where(active, table[0:1], -1), jnp.where(active, table[1:2], -1)], 1)
    turn = table[2:3]
    fhot_ref = t["fhot"]
    put_one_hot(fhot_ref, ids, iota_ref, NF)
    code, slots = v["code"][...], v["slot"][...]
    v["idr"][...] = jnp.full_like(v["idr"], -1)
    ones = jnp.ones((16, NE), BF16)
    for f in range(NF):
        listed = dot_t(ones, fhot_ref[f * NE : (f + 1) * NE, :])[0:1] > 0.5
        t["free"][f : f + 1, :] = jnp.where(listed, 0.0, 1.0)
        slot = slots[f : f + 1]
        remote = slot >= NE
        v["idr"][f : f + 1, :] = jnp.where(remote & ~listed, slot - NE, -1)
        own_id = (code[f : f + 1] // 3) * NE + slot
        t["ids"][f : f + 1, :] = jnp.where(remote | listed, -1, own_id)
    send("idr")
    send_face = copies.reserve([("g", f) for f in range(NF)], v["g"], hbm["g"])

    def by_face(f, i):
        put_one_hot(hot_ref, t["ids"][f : f + 1, :], iota_ref, NF)
        v["g"][f] = picked(hot_ref)
        for h in range(2):
            acc = mix_flux(tr_ref, v["own"], f, HALVES[h])
            keep = t["free"][f : f + 1, HALVES[h]]
            for q in range(NQ):
                t["st"][f, q * MP : (q + 1) * MP, HALVES[h]] = keep * acc[q]

        send_face(i)

    one_by_one(NF, by_face)


    for q in range(NQ):
        rows = slice(q * MP, (q + 1) * MP)
        state = jnp.concatenate([t["st"][f, rows, :] for f in range(NF)], 0)
        hi, lo = split(state)
        part_ref[q] = part_ref[q] - dot(pt_ref[...], jnp.concatenate([hi, hi, lo], 0))
    send("part")
    wf_ref, rw_ref, rtw_ref = v["wf"], t["rw"], v["rtw"]
    copies.wait("rot")
    wf_ref[...] = jnp.zeros_like(wf_ref)
    rw_ref[...] = jnp.zeros_like(rw_ref)
    rtw_ref[...] = jnp.zeros_like(rtw_ref)
    rots = [split(v["rot"][h]) for h in range(3)]
    for h in range(3):
        rw_ref[0, h * MP : h * MP + NM, 0:NM] = rots[h][0]
        rw_ref[1, h * MP : h * MP + NM, 0:NM] = rots[h][1]
        hi, lo = split(v["rot"][h].T)
        rtw_ref[0, h * MP : h * MP + NM, 0:NM] = hi
        rtw_ref[1, h * MP : h * MP + NM, 0:NM] = lo
    for f in range(NF):
        turn_over = v["proj"][:, f, :].T
        hi, lo = split(turn_over)
        for h in range(3):
            rhi, rlo = rots[h]
            whi, wlo = split(dot(hi, rhi) + dot(lo, rhi) + dot(hi, rlo))
            at = h * 96 + f * MP
            wf_ref[:, at : at + NM] = whi
            wf_ref[:, 288 + at : 288 + at + NM] = wlo
            wf_ref[:, 576 + at : 576 + at + NM] = whi
    send("wf")
    send("rtw")
    t["raw"][...] = picked(fhot_ref)
    raw = jnp.concatenate([t["raw"][q * MP : (q + 1) * MP, NS:] for q in range(NQ)], 1)
    ts[0][0:72, :] = turned(rw_ref, raw)
    for q in range(NQ):
        rows = slice(q * MP, (q + 1) * MP)
        v["pair"][rows, :NS] = t["raw"][rows, :NS]
        v["pair"][rows, NS:] = choose(ts[0], turn, q)
    send("pair")
    copies.finish()


def turned(w_ref, x):
    hi, lo = split(x)
    return dot(w_ref[0], hi) + dot(w_ref[1], hi) + dot(w_ref[0], lo)


def choose(ref, turn, q):
    out = jnp.zeros((MP, NS), F32)
    for h in range(3):
        piece = ref[h * MP : (h + 1) * MP, q * NS : (q + 1) * NS]
        out = jnp.where(turn == h, piece, out)
    return out


FAR_IN = ("table", "code", "idr", "params", "rtw", "pair", "pt", "r0", "r1", "r2", "r3", "flux", "g", "wf", "part")
FAR_TMP = ("gs", "z", "mask", "hot", "ehot", "iota", "ph", "pl", "scr", "fs", "back", "lift")
FAR_COPIES = 14 + NF + NQ


def far_kernel(*refs):
    ni = len(FAR_IN)
    hbm = named(FAR_IN + ("out",), refs[: ni + 1])
    v = named(FAR_IN + ("out",), refs[ni + 1 : 2 * ni + 2])
    t = named(FAR_TMP, refs[2 * ni + 2 : -1])
    copies = Copies(refs[-1])
    for name in FAR_IN:
        if name != "g":
            copies.start(name, hbm[name], v[name])
    first = copies.count
    copies.count += NF

    def g_copy(i):
        return copies.made(hbm["g"], v["g"], i, first + i)

    for f in range(NF):
        g_copy(f).start()
    iota_ref = t["iota"]
    put_iota(iota_ref)
    copies.wait("table")
    table = v["table"][...]
    active = table[0:1] >= 0
    ids = jnp.concatenate([jnp.where(active, table[0:1], -1), jnp.where(active, table[1:2], -1)], 1)
    turn = table[2:3]
    copies.wait("code", "idr")
    code = v["code"][...] % 3
    for h in range(3):
        rows = [
            jnp.broadcast_to(jnp.where(code[f : f + 1] == h, 1.0, 0.0), (MP, NE))
            for f in range(NF)
        ]
        t["mask"][h] = jnp.concatenate(rows, 0).astype(BF16)
    copies.wait("params", "rtw", "pair", "pt")
    scr, pair, fs = t["scr"], v["pair"], t["fs"]
    scr[0:128, :] = v["params"][:, 0, :].T
    scr[128:256, :] = v["params"][:, 1, :].T
    eta = scr[ETA_ROW : ETA_ROW + 1, :]
    ratio = eta / (1.0 + eta)

    def param(row):
        return jnp.broadcast_to(scr[pl.ds(row, 1), :], (MP, NS))

    def by_quantity(q, c):
        a = b = None
        for p in range(NQ):
            g, hh = param(p * NQ + q), param(PLUS_ROW + p * NQ + q)
            near = pair[p * MP : (p + 1) * MP, :NS]
            far = pair[p * MP : (p + 1) * MP, NS:]
            x = near * g + far * hh
            y = far * g + near * hh
            a = x if a is None else a + x
            b = y if b is None else b + y
        rows = pl.ds(pl.multiple_of(q * MP, 8), MP)
        slip = jnp.where(q >= 3, ratio, 0.0) * (pair[rows, NS:] - pair[rows, :NS])
        fs[rows, :NS] = a + slip
        fs[rows, NS:] = b - slip
        return c

    lax.fori_loop(0, NQ, by_quantity, 0)
    raw = jnp.concatenate([fs[q * MP : (q + 1) * MP, NS:] for q in range(NQ)], 1)
    t["back"][...] = turned(v["rtw"], raw)
    for q in range(NQ):
        fs[q * MP : (q + 1) * MP, NS:] = choose(t["back"], turn, q)
    face = ids >> 8
    for q in range(NQ):
        x = fs[q * MP : (q + 1) * MP, :]
        tall = jnp.concatenate([jnp.where(face == f, x, 0.0) for f in range(NF)], 0)
        hi, lo = split(tall)
        t["lift"][q * NB : (q + 1) * NB, :] = dot(v["pt"][...], jnp.concatenate([hi, hi, lo], 0))
    ehot_ref = t["ehot"]
    put_one_hot(ehot_ref, jnp.where(ids >= 0, ids & (NE - 1), -1), iota_ref, 1)
    hi, lo = split(t["lift"][...])
    hot = ehot_ref[...]
    t["lift"][...] = dot_t(hi, hot) + dot_t(lo, hot)
    hot_ref = t["hot"]
    copies.wait("r0", "r1", "r2", "r3")
    ph_ref, pl_ref = t["ph"], t["pl"]
    for o in range(NF):
        hi, lo = split(v[f"r{o}"][...])
        ph_ref[:, o * NS : (o + 1) * NS] = hi
        pl_ref[:, o * NS : (o + 1) * NS] = lo
    copies.wait("flux")
    gs_ref = t["gs"]

    def by_face(f, i):
        put_one_hot(hot_ref, v["idr"][f : f + 1, :], iota_ref, 2)
        g_copy(i).wait()
        gs_ref[f] = v["g"][f] + dot(ph_ref[...], hot_ref[...]) + dot(pl_ref[...], hot_ref[...])
        for h in range(2):
            acc = mix_flux(gs_ref, v["flux"], f, HALVES[h])
            for q in range(NQ):
                t["z"][q, f * MP : (f + 1) * MP, HALVES[h]] = acc[q]

    one_by_one(NF, by_face)
    copies.wait("wf", "part")
    send_quantity = copies.reserve([("out", q) for q in range(NQ)], v["out"], hbm["out"])

    def by_quantity(part, i):
        for q in range(3 * part, 3 * part + 3):
            hi, lo = split(t["z"][q])
            his = [hi * t["mask"][h] for h in range(3)]
            los = [lo * t["mask"][h] for h in range(3)]
            lifted = dot(v["wf"][...], jnp.concatenate(his + his + los, 0))
            v["out"][q] = v["part"][q] - t["lift"][q * NB : (q + 1) * NB, :] - lifted
            send_quantity(3 * i + q - 3 * part)

    one_by_one(3, by_quantity)
    copies.finish()


def sds(shape, dtype=F32):
    return jax.ShapeDtypeStruct(shape, dtype)


def shifted(block, distance):
    n = lax.axis_size("dom")
    return lax.ppermute(block, "dom", [((i - distance) % n, i) for i in range(n)])


V = pltpu.VMEM
VMEM_LIMIT = 67043328
IN_HBM = pl.BlockSpec(memory_space=pl.ANY)
DMA = pltpu.SemaphoreType.DMA


def held(arrays):
    return [V(a.shape, a.dtype) for a in arrays]


def call(kernel, ins, out, scratch):
    return pl.pallas_call(
        kernel,
        out_shape=out,
        in_specs=[IN_HBM] * len(ins),
        out_specs=[IN_HBM] * len(out),
        scratch_shapes=scratch,
        compiler_params=pltpu.CompilerParams(vmem_limit_bytes=VMEM_LIMIT),
        cost_estimate=pl.CostEstimate(flops=10**8, bytes_accessed=3 * 10**6, transcendentals=0),
    )(*ins)


def shards(
    coefficients, star_matrices, own_flux, neighbour_flux, stiffness, projection, rotation,
    fault_minus, fault_plus, slip_compliance, neighbour_slot, neighbour_code, halo_send, fault_table,
):
    coef = jnp.transpose(coefficients, (1, 0, 2))
    star = jnp.transpose(star_matrices, (1, 2, 0, 3))
    proj = jnp.transpose(projection, (1, 0, 2))
    t_half = V((3 * NB, QL), F32)
    w_stiff = V((3 * NB, 3 * BP), BF16)
    iota = V((NE, NE), BF16)
    hot = V((NF * NE, NE), BF16)
    flat = V((RT, NF * NE), BF16)
    turn = (2, 72, MP)
    eta = slip_compliance.reshape(1, -1)
    ins = [stiffness, proj, coef, star, fault_minus, fault_plus, eta, halo_send]
    outs = [
        sds((128, 2, 128)), *[sds((2 * BP, QL), BF16)] * 2, sds((NF, RT, NE)),
        *[sds((RT, NF * NE), BF16)] * 2, *[sds((RT, NS))] * 4,
    ]
    packed, xs0, xs1, tr, th, tl, *pays = call(
        first_kernel, ins, outs,
        [
            *held(ins), *held(outs), t_half, t_half, w_stiff, V((NQ, NB, NE), F32),
            V((NF * MP, 3 * BP), BF16), hot, hot, iota, V((256, 128), F32),
            DMA((FIRST_COPIES,)),
        ],
    )
    params = lax.all_to_all(packed, "dom", 0, 0, tiled=True)
    arrived = []
    for o in range(4):
        arrived.append(shifted(pays[o], SHIFTS[o]))
    ins = [
        stiffness, proj, xs0, xs1, star, coef, fault_table, neighbour_slot, neighbour_code,
        rotation, th, tl, tr, own_flux,
    ]
    outs = [
        sds((NQ, NB, NE)), sds((NF, RT, NE)), sds((RT, NE)), sds((NB, 864), BF16),
        sds((NB, 288), BF16), sds(turn, BF16), sds((8, NE), jnp.int32),
    ]
    part, g, pair, wf, pt, rtw, idr = call(
        near_kernel, ins, outs,
        [
            *held(ins), *held(outs), t_half, t_half, w_stiff, hot, iota,
            V((NF, RT, NE), F32), hot, V((RT, NE), F32), V((8, NE), F32),
            V((8, NE), jnp.int32), V(turn, BF16), DMA((NEAR_COPIES,)),
        ],
    )
    ins = [
        fault_table, neighbour_code, idr, params, rtw, pair, pt, *arrived, neighbour_flux, g, wf, part
    ]
    outs = [sds((NQ, NB, NE))]
    (out,) = call(
        far_kernel, ins, outs,
        [
            *held(ins), *held(outs),
            V((NF, RT, NE), F32), V((NQ, NF * MP, NE), F32), V((3, NF * MP, NE), BF16),
            V((2 * NE, NE), BF16), V((NE, NE), BF16), iota, V((RT, 4 * NS), BF16),
            V((RT, 4 * NS), BF16), V((256, 128), F32), V((RT, NE), F32), V((72, QL), F32),
            V((NQ * NB, NE), F32), DMA((FAR_COPIES,)),
        ],
    )
    return jnp.transpose(out, (1, 0, 2))


def solution(mesh):
    e3, e4 = P(None, None, "dom"), P(None, None, None, "dom")
    row = P(None, "dom")
    placed = (e3, e4, e4, e4, P(), P(), P(), e3, e3, P("dom"), row, row, row, row)
    return jax.shard_map(shards, mesh=mesh, in_specs=placed, out_specs=e3, check_vma=False)
```

profile of v0, /device:TPU:0, one launch (start us, length us, event | category | flops | bytes accessed | tf_op | source)
XLA Modules:
  0.0 45.0 jit_solution(9448688974233551513)
XLA Ops:
  0.0 10.6 %shard_map.136 = (f32[128,2,128]{2,1,0:T(2,128)}, bf16[128,1152]{1,0:T(8,128)(2,1)}, bf16[128,1152]{1,0:T(8,128)(2,1)}, f32[4,216,256]{2,1,0:T(8,128)}, bf16[216...) custom-call(f32[3,56,56]{2,1,0:T(8,128)} %refs_0_.4, ...), custom_call_target="tpu_custom_call" | custom-call | flops 100000000 | bytes 3000000 | tf_op jit(solution)/shard_map/pallas_call | solution.py:537
  10.6 11.7 %all-to-all-start = ((f32[128,2,128]{2,1,0:T(2,128)}), f32[128,2,128]{2,1,0:T(2,128)}, u32[]{:S(2)}, u32[]{:S(2)}) async-start(f32[128,2,128]{2,1,0:T(2,128)} %get-tuple-element.28), calls=%async_computation | async-start | bytes 262144 | tf_op jit(solution)/shard_map/all_to_all | solution.py:575
  22.3 0.1 collective-permute-start
  22.4 1.1 %collective-permute-start.1 = (f32[216,128]{1,0:T(8,128)}, f32[216,128]{1,0:T(8,128)}, u32[]{:S(2)}, u32[]{:S(2)}) collective-permute-start(f32[216,128]{1,0:T(8,128)} %get-tuple-element.33), channel_id=1, source_target_pairs={{126,0},{127,1},{0,2},{1,3},{2,4},{3,5},{4,6},{5,7},{6,8},{7,9},{8... | collective-permute-start | bytes 331784 | tf_op jit(solution)/shard_map/ppermute | solution.py:523
  23.5 6.8 %collective-permute-start.2 = (f32[216,128]{1,0:T(8,128)}, f32[216,128]{1,0:T(8,128)}, u32[]{:S(2)}, u32[]{:S(2)}) collective-permute-start(f32[216,128]{1,0:T(8,128)} %get-tuple-element.34), channel_id=1, source_target_pairs={{1,0},{2,1},{3,2},{4,3},{5,4},{6,5},{7,6},{8,7},{9,8},{10,9},{11,1... | collective-permute-start | bytes 331784 | tf_op jit(solution)/shard_map/ppermute | solution.py:523
  30.3 1.1 %collective-permute-start.3 = (f32[216,128]{1,0:T(8,128)}, f32[216,128]{1,0:T(8,128)}, u32[]{:S(2)}, u32[]{:S(2)}) collective-permute-start(f32[216,128]{1,0:T(8,128)} %get-tuple-element.35), channel_id=1, source_target_pairs={{2,0},{3,1},{4,2},{5,3},{6,4},{7,5},{8,6},{9,7},{10,8},{11,9},{12,... | collective-permute-start | bytes 331784 | tf_op jit(solution)/shard_map/ppermute | solution.py:523
  31.3 7.3 %shard_map.137 = (f32[9,56,256]{2,1,0:T(8,128)}, f32[4,216,256]{2,1,0:T(8,128)}, f32[216,256]{1,0:T(8,128)}, bf16[56,864]{1,0:T(8,128)(2,1)}, bf16[56,288]{1,0:T...) custom-call(f32[3,56,56]{2,1,0:T(8,128)} %refs_0_.4, f32[21,4,56]{2,1,0:T(4,128)} %bitcast.10, ...), custom_call_target="tpu_custom_call" | custom-call | flops 100000000 | bytes 3000000 | tf_op jit(solution)/shard_map/pallas_call | solution.py:537
  38.7 0.0 collective-permute-done.refs_7_
  38.7 0.0 collective-permute-done.1.refs_8_
  38.7 0.0 collective-permute-done.2.refs_9_
  38.7 0.0 collective-permute-done.3.refs_10_
  38.7 0.0 all-to-all-done.refs_3_
  38.7 6.2 %shard_map.138 = f32[9,56,256]{2,1,0:T(8,128)} custom-call(s32[3,128]{1,0:T(4,128)} %refs_0_.5, s32[4,256]{1,0:T(4,128)} %refs_1_.1, s32[8,256]{1,0:T(8,128)} %get-tuple-element.27.refs_2_, f32[128,2,128]{2,1,0:T(2,128)} %all-to-all-done.refs_3_, bf16[2,72,24]{2,1,0:T(8,128)(2,1)} %get-tuple-element.29.refs_4_, f32[216,256]{1,0:T(8,128)} %get-tuple-element.30.refs_5_, ...), custom_call_target="tpu_custom_call" | custom-call | flops 100000000 | bytes 3000000 | tf_op jit(solution)/shard_map/pallas_call | solution.py:537
Async XLA Ops:
  10.6 28.2 %all-to-all-start = ((f32[128,2,128]{2,1,0:T(2,128)}), f32[128,2,128]{2,1,0:T(2,128)}, u32[]{:S(2)}, u32[]{:S(2)}) async-start(f32[128,2,128]{2,1,0:T(2,128)} %get-tuple-element.28), calls=%async_computation | async-start | bytes 262144 | tf_op jit(solution)/shard_map/all_to_all | solution.py:575
  22.3 16.4 %collective-permute-start = (f32[216,128]{1,0:T(8,128)}, f32[216,128]{1,0:T(8,128)}, u32[]{:S(2)}, u32[]{:S(2)}) collective-permute-start(f32[216,128]{1,0:T(8,128)} %get-tuple-element.32), channel_id=1, source_target_pairs={{127,0},{0,1},{1,2},{2,3},{3,4},{4,5},{5,6},{6,7},{7,8},{8,9},{9,1... | collective-permute-start | bytes 331784 | tf_op jit(solution)/shard_map/ppermute | solution.py:523
  22.4 16.3 %collective-permute-start.1 = (f32[216,128]{1,0:T(8,128)}, f32[216,128]{1,0:T(8,128)}, u32[]{:S(2)}, u32[]{:S(2)}) collective-permute-start(f32[216,128]{1,0:T(8,128)} %get-tuple-element.33), channel_id=1, source_target_pairs={{126,0},{127,1},{0,2},{1,3},{2,4},{3,5},{4,6},{5,7},{6,8},{7,9},{8... | collective-permute-start | bytes 331784 | tf_op jit(solution)/shard_map/ppermute | solution.py:523
  23.5 15.2 %collective-permute-start.2 = (f32[216,128]{1,0:T(8,128)}, f32[216,128]{1,0:T(8,128)}, u32[]{:S(2)}, u32[]{:S(2)}) collective-permute-start(f32[216,128]{1,0:T(8,128)} %get-tuple-element.34), channel_id=1, source_target_pairs={{1,0},{2,1},{3,2},{4,3},{5,4},{6,5},{7,6},{8,7},{9,8},{10,9},{11,1... | collective-permute-start | bytes 331784 | tf_op jit(solution)/shard_map/ppermute | solution.py:523
  30.3 8.4 %collective-permute-start.3 = (f32[216,128]{1,0:T(8,128)}, f32[216,128]{1,0:T(8,128)}, u32[]{:S(2)}, u32[]{:S(2)}) collective-permute-start(f32[216,128]{1,0:T(8,128)} %get-tuple-element.35), channel_id=1, source_target_pairs={{2,0},{3,1},{4,2},{5,3},{6,4},{7,5},{8,6},{9,7},{10,8},{11,9},{12,... | collective-permute-start | bytes 331784 | tf_op jit(solution)/shard_map/ppermute | solution.py:523
where the time goes:
time: 45.2 us; the launch traced here: 45 us
  Pallas kernels  24.1 us (53%)
  starting transfers between devices  20.8 us (46%)
    pallas_call x3, Pallas kernels, call(): pl.pallas_call(kernel, out_shape=out, in_specs=[IN_HBM] * len(ins), out_s...  24.1 us
    all_to_all x1, starting transfers between devices, shards(): params = lax.all_to_all(packed, 'dom', 0, 0, tiled=True)  11.7 us
    ppermute x4, starting transfers between devices, shifted(): lax.ppermute(block, 'dom', [((i - distance) % n, i) for i in range(n)])  9.04 us
  transfers between devices with their start and end apart: 5, of which 0 were waited for; matrix products, arithmetic and copies ran while one was open for 0% of the time, Pallas kernels for 16%

commit v1 on v0

--- a/solution.py
+++ b/solution.py
@@ -259,10 +259,10 @@
     copies.finish()
 
 
-NEAR_IN = ("stiff", "proj", "xs0", "xs1", "star", "coef", "table", "slot", "code", "rot", "th", "tl", "tr", "own")
-NEAR_OUT = ("part", "g", "pair", "wf", "pt", "rtw", "idr")
-NEAR_TMP = ("t0", "t1", "wv", "hot", "iota", "st", "fhot", "raw", "free", "ids", "rw")
-NEAR_COPIES = 14 + 6 + 4
+NEAR_IN = ("stiff", "proj", "xs0", "xs1", "star", "coef", "table", "slot", "code", "rot", "th", "tl", "tr", "own", "r0", "r1", "r2", "r3", "flux")
+NEAR_OUT = ("part", "pair", "pt", "rtw")
+NEAR_TMP = ("t0", "t1", "wv", "hot", "iota", "st", "fhot", "raw", "free", "ids", "rw", "wf", "idr", "g", "z", "mask", "rhot", "ph", "pl")
+NEAR_COPIES = 19 + 3 + NQ
 
 
 def near_kernel(*refs):
@@ -318,40 +318,16 @@
     fhot_ref = t["fhot"]
     put_one_hot(fhot_ref, ids, iota_ref, NF)
     code, slots = v["code"][...], v["slot"][...]
-    v["idr"][...] = jnp.full_like(v["idr"], -1)
     ones = jnp.ones((16, NE), BF16)
     for f in range(NF):
         listed = dot_t(ones, fhot_ref[f * NE : (f + 1) * NE, :])[0:1] > 0.5
         t["free"][f : f + 1, :] = jnp.where(listed, 0.0, 1.0)
         slot = slots[f : f + 1]
         remote = slot >= NE
-        v["idr"][f : f + 1, :] = jnp.where(remote & ~listed, slot - NE, -1)
+        t["idr"][f : f + 1, :] = jnp.where(remote & ~listed, slot - NE, -1)
         own_id = (code[f : f + 1] // 3) * NE + slot
         t["ids"][f : f + 1, :] = jnp.where(remote | listed, -1, own_id)
-    send("idr")
-    send_face = copies.reserve([("g", f) for f in range(NF)], v["g"], hbm["g"])
-
-    def by_face(f, i):
-        put_one_hot(hot_ref, t["ids"][f : f + 1, :], iota_ref, NF)
-        v["g"][f] = picked(hot_ref)
-        for h in range(2):
-            acc = mix_flux(tr_ref, v["own"], f, HALVES[h])
-            keep = t["free"][f : f + 1, HALVES[h]]
-            for q in range(NQ):
-                t["st"][f, q * MP : (q + 1) * MP, HALVES[h]] = keep * acc[q]
-
-        send_face(i)
-
-    one_by_one(NF, by_face)
-
-
-    for q in range(NQ):
-        rows = slice(q * MP, (q + 1) * MP)
-        state = jnp.concatenate([t["st"][f, rows, :] for f in range(NF)], 0)
-        hi, lo = split(state)
-        part_ref[q] = part_ref[q] - dot(pt_ref[...], jnp.concatenate([hi, hi, lo], 0))
-    send("part")
-    wf_ref, rw_ref, rtw_ref = v["wf"], t["rw"], v["rtw"]
+    wf_ref, rw_ref, rtw_ref = t["wf"], t["rw"], v["rtw"]
     copies.wait("rot")
     wf_ref[...] = jnp.zeros_like(wf_ref)
     rw_ref[...] = jnp.zeros_like(rw_ref)
@@ -373,7 +349,6 @@
             wf_ref[:, at : at + NM] = whi
             wf_ref[:, 288 + at : 288 + at + NM] = wlo
             wf_ref[:, 576 + at : 576 + at + NM] = whi
-    send("wf")
     send("rtw")
     t["raw"][...] = picked(fhot_ref)
     raw = jnp.concatenate([t["raw"][q * MP : (q + 1) * MP, NS:] for q in range(NQ)], 1)
@@ -383,6 +358,56 @@
         v["pair"][rows, :NS] = t["raw"][rows, :NS]
         v["pair"][rows, NS:] = choose(ts[0], turn, q)
     send("pair")
+    copies.wait("r0", "r1", "r2", "r3", "flux")
+    ph_ref, pl_ref = t["ph"], t["pl"]
+    for o in range(NF):
+        hi, lo = split(v[f"r{o}"][...])
+        ph_ref[:, o * NS : (o + 1) * NS] = hi
+        pl_ref[:, o * NS : (o + 1) * NS] = lo
+    way = code % 3
+    for h in range(3):
+        rows = [
+            jnp.broadcast_to(jnp.where(way[f : f + 1] == h, 1.0, 0.0), (MP, NE))
+            for f in range(NF)
+        ]
+        t["mask"][h] = jnp.concatenate(rows, 0).astype(BF16)
+    rhot_ref, g_ref = t["rhot"], t["g"]
+
+    def by_face(f, i):
+        put_one_hot(hot_ref, t["ids"][f : f + 1, :], iota_ref, NF)
+        put_one_hot(rhot_ref, t["idr"][f : f + 1, :], iota_ref, 2)
+        for h in range(2):
+            acc = mix_flux(tr_ref, v["own"], f, HALVES[h])
+            keep = t["free"][f : f + 1, HALVES[h]]
+            for q in range(NQ):
+                t["st"][f, q * MP : (q + 1) * MP, HALVES[h]] = keep * acc[q]
+        here = picked(hot_ref)
+        g_ref[f] = here + (dot(ph_ref[...], rhot_ref[...]) + dot(pl_ref[...], rhot_ref[...]))
+
+    def by_far_face(f, i):
+        for h in range(2):
+            acc = mix_flux(g_ref, v["flux"], f, HALVES[h])
+            for q in range(NQ):
+                t["z"][q, f * MP : (f + 1) * MP, HALVES[h]] = acc[q]
+
+    one_by_one(NF, by_face)
+    one_by_one(NF, by_far_face)
+    send_part = copies.reserve([("part", q) for q in range(NQ)], part_ref, hbm["part"])
+
+    def by_quantity(part, i):
+        for q in range(3 * part, 3 * part + 3):
+            rows = slice(q * MP, (q + 1) * MP)
+            state = jnp.concatenate([t["st"][f, rows, :] for f in range(NF)], 0)
+            hi, lo = split(state)
+            own = dot(pt_ref[...], jnp.concatenate([hi, hi, lo], 0))
+            hi, lo = split(t["z"][q])
+            his = [hi * t["mask"][h] for h in range(3)]
+            los = [lo * t["mask"][h] for h in range(3)]
+            far = dot(t["wf"][...], jnp.concatenate(his + his + los, 0))
+            part_ref[q] = part_ref[q] - own - far
+            send_part(3 * i + q - 3 * part)
+
+    one_by_one(3, by_quantity)
     copies.finish()
 
 
@@ -399,9 +424,9 @@
     return out
 
 
-FAR_IN = ("table", "code", "idr", "params", "rtw", "pair", "pt", "r0", "r1", "r2", "r3", "flux", "g", "wf", "part")
-FAR_TMP = ("gs", "z", "mask", "hot", "ehot", "iota", "ph", "pl", "scr", "fs", "back", "lift")
-FAR_COPIES = 14 + NF + NQ
+FAR_IN = ("table", "params", "rtw", "pair", "pt", "part")
+FAR_TMP = ("ehot", "iota", "scr", "fs", "back", "lift")
+FAR_COPIES = 6 + NQ
 
 
 def far_kernel(*refs):
@@ -411,16 +436,7 @@
     t = named(FAR_TMP, refs[2 * ni + 2 : -1])
     copies = Copies(refs[-1])
     for name in FAR_IN:
-        if name != "g":
-            copies.start(name, hbm[name], v[name])
-    first = copies.count
-    copies.count += NF
-
-    def g_copy(i):
-        return copies.made(hbm["g"], v["g"], i, first + i)
-
-    for f in range(NF):
-        g_copy(f).start()
+        copies.start(name, hbm[name], v[name])
     iota_ref = t["iota"]
     put_iota(iota_ref)
     copies.wait("table")
@@ -428,14 +444,6 @@
     active = table[0:1] >= 0
     ids = jnp.concatenate([jnp.where(active, table[0:1], -1), jnp.where(active, table[1:2], -1)], 1)
     turn = table[2:3]
-    copies.wait("code", "idr")
-    code = v["code"][...] % 3
-    for h in range(3):
-        rows = [
-            jnp.broadcast_to(jnp.where(code[f : f + 1] == h, 1.0, 0.0), (MP, NE))
-            for f in range(NF)
-        ]
-        t["mask"][h] = jnp.concatenate(rows, 0).astype(BF16)
     copies.wait("params", "rtw", "pair", "pt")
     scr, pair, fs = t["scr"], v["pair"], t["fs"]
     scr[0:128, :] = v["params"][:, 0, :].T
@@ -477,40 +485,11 @@
     put_one_hot(ehot_ref, jnp.where(ids >= 0, ids & (NE - 1), -1), iota_ref, 1)
     hi, lo = split(t["lift"][...])
     hot = ehot_ref[...]
-    t["lift"][...] = dot_t(hi, hot) + dot_t(lo, hot)
-    hot_ref = t["hot"]
-    copies.wait("r0", "r1", "r2", "r3")
-    ph_ref, pl_ref = t["ph"], t["pl"]
-    for o in range(NF):
-        hi, lo = split(v[f"r{o}"][...])
-        ph_ref[:, o * NS : (o + 1) * NS] = hi
-        pl_ref[:, o * NS : (o + 1) * NS] = lo
-    copies.wait("flux")
-    gs_ref = t["gs"]
-
-    def by_face(f, i):
-        put_one_hot(hot_ref, v["idr"][f : f + 1, :], iota_ref, 2)
-        g_copy(i).wait()
-        gs_ref[f] = v["g"][f] + dot(ph_ref[...], hot_ref[...]) + dot(pl_ref[...], hot_ref[...])
-        for h in range(2):
-            acc = mix_flux(gs_ref, v["flux"], f, HALVES[h])
-            for q in range(NQ):
-                t["z"][q, f * MP : (f + 1) * MP, HALVES[h]] = acc[q]
-
-    one_by_one(NF, by_face)
-    copies.wait("wf", "part")
-    send_quantity = copies.reserve([("out", q) for q in range(NQ)], v["out"], hbm["out"])
-
-    def by_quantity(part, i):
-        for q in range(3 * part, 3 * part + 3):
-            hi, lo = split(t["z"][q])
-            his = [hi * t["mask"][h] for h in range(3)]
-            los = [lo * t["mask"][h] for h in range(3)]
-            lifted = dot(v["wf"][...], jnp.concatenate(his + his + los, 0))
-            v["out"][q] = v["part"][q] - t["lift"][q * NB : (q + 1) * NB, :] - lifted
-            send_quantity(3 * i + q - 3 * part)
-
-    one_by_one(3, by_quantity)
+    copies.wait("part")
+    for q in range(NQ):
+        rows = slice(q * NB, (q + 1) * NB)
+        v["out"][q] = v["part"][q] - (dot_t(hi[rows], hot) + dot_t(lo[rows], hot))
+        copies.start(("out", q), v["out"], hbm["out"], q)
     copies.finish()
 
 
@@ -578,32 +557,27 @@
         arrived.append(shifted(pays[o], SHIFTS[o]))
     ins = [
         stiffness, proj, xs0, xs1, star, coef, fault_table, neighbour_slot, neighbour_code,
-        rotation, th, tl, tr, own_flux,
+        rotation, th, tl, tr, own_flux, *arrived, neighbour_flux,
     ]
-    outs = [
-        sds((NQ, NB, NE)), sds((NF, RT, NE)), sds((RT, NE)), sds((NB, 864), BF16),
-        sds((NB, 288), BF16), sds(turn, BF16), sds((8, NE), jnp.int32),
-    ]
-    part, g, pair, wf, pt, rtw, idr = call(
+    outs = [sds((NQ, NB, NE)), sds((RT, NE)), sds((NB, 288), BF16), sds(turn, BF16)]
+    part, pair, pt, rtw = call(
         near_kernel, ins, outs,
         [
             *held(ins), *held(outs), t_half, t_half, w_stiff, hot, iota,
             V((NF, RT, NE), F32), hot, V((RT, NE), F32), V((8, NE), F32),
-            V((8, NE), jnp.int32), V(turn, BF16), DMA((NEAR_COPIES,)),
+            V((8, NE), jnp.int32), V(turn, BF16), V((NB, 864), BF16),
+            V((8, NE), jnp.int32), V((NF, RT, NE), F32), V((NQ, NF * MP, NE), F32),
+            V((3, NF * MP, NE), BF16), V((2 * NE, NE), BF16), V((RT, 4 * NS), BF16),
+            V((RT, 4 * NS), BF16), DMA((NEAR_COPIES,)),
         ],
     )
-    ins = [
-        fault_table, neighbour_code, idr, params, rtw, pair, pt, *arrived, neighbour_flux, g, wf, part
-    ]
+    ins = [fault_table, params, rtw, pair, pt, part]
     outs = [sds((NQ, NB, NE))]
     (out,) = call(
         far_kernel, ins, outs,
         [
-            *held(ins), *held(outs),
-            V((NF, RT, NE), F32), V((NQ, NF * MP, NE), F32), V((3, NF * MP, NE), BF16),
-            V((2 * NE, NE), BF16), V((NE, NE), BF16), iota, V((RT, 4 * NS), BF16),
-            V((RT, 4 * NS), BF16), V((256, 128), F32), V((RT, NE), F32), V((72, QL), F32),
-            V((NQ * NB, NE), F32), DMA((FAR_COPIES,)),
+            *held(ins), *held(outs), V((NE, NE), BF16), iota, V((256, 128), F32),
+            V((RT, NE), F32), V((72, QL), F32), V((NQ * NB, NE), F32), DMA((FAR_COPIES,)),
         ],
     )
     return jnp.transpose(out, (1, 0, 2))

time: 45.2 us -> 49.7 us (1.100)
  waiting for transfers between devices: 0.01 us -> 3.78 us
    ppermute x4, waiting for transfers between devices: 0.01 us -> 3.78 us  [shifted(): lax.ppermute(block, 'dom', [((i - distance) % n, i) for i in range(n)])]
  transfers between devices with their start and end apart: 5 -> 5, of which waited for: 0 -> 3; matrix products, arithmetic and copies ran while one was open for 0% -> 0% of each run, Pallas kernels for 16% -> 20%
where the time goes in v1:
time: 49.7 us; the launch traced here: 49.1 us
  Pallas kernels  24.3 us (49%)
  starting transfers between devices  20.7 us (42%)
  waiting for transfers between devices  3.78 us (8%)
    pallas_call x3, Pallas kernels, call(): pl.pallas_call(kernel, out_shape=out, in_specs=[IN_HBM] * len(ins), out_s...  24.3 us
    all_to_all x1, starting transfers between devices, shards(): params = lax.all_to_all(packed, 'dom', 0, 0, tiled=True)  11.7 us
    ppermute x4, starting transfers between devices, shifted(): lax.ppermute(block, 'dom', [((i - distance) % n, i) for i in range(n)])  9.04 us
    ppermute x4, waiting for transfers between devices, shifted(): lax.ppermute(block, 'dom', [((i - distance) % n, i) for i in range(n)])  3.78 us
  transfers between devices with their start and end apart: 5, of which 3 were waited for; matrix products, arithmetic and copies ran while one was open for 0% of the time, Pallas kernels for 20%

profile of v1, /device:TPU:0, one launch (start us, length us, event | category | flops | bytes accessed | tf_op | source)
XLA Modules:
  0.0 49.1 jit_solution(16529608064854380201)
XLA Ops:
  0.0 10.6 %shard_map.136 = (f32[128,2,128]{2,1,0:T(2,128)}, bf16[128,1152]{1,0:T(8,128)(2,1)}, bf16[128,1152]{1,0:T(8,128)(2,1)}, f32[4,216,256]{2,1,0:T(8,128)}, bf16[216...) custom-call(f32[3,56,56]{2,1,0:T(8,128)} %refs_0_.4, ...), custom_call_target="tpu_custom_call" | custom-call | flops 100000000 | bytes 3000000 | tf_op jit(solution)/shard_map/pallas_call | solution.py:516
  10.6 0.0 copy-start.1
  10.6 0.0 copy-start
  10.6 11.7 %all-to-all-start = ((f32[128,2,128]{2,1,0:T(2,128)}), f32[128,2,128]{2,1,0:T(2,128)}, u32[]{:S(2)}, u32[]{:S(2)}) async-start(f32[128,2,128]{2,1,0:T(2,128)} %get-tuple-element.19), calls=%async_computation | async-start | bytes 262144 | tf_op jit(solution)/shard_map/all_to_all | solution.py:554
  22.3 0.1 collective-permute-start
  22.4 1.1 %collective-permute-start.1 = (f32[216,128]{1,0:T(8,128)}, f32[216,128]{1,0:T(8,128)}, u32[]{:S(2)}, u32[]{:S(2)}) collective-permute-start(f32[216,128]{1,0:T(8,128)} %get-tuple-element.26), channel_id=1, source_target_pairs={{126,0},{127,1},{0,2},{1,3},{2,4},{3,5},{4,6},{5,7},{6,8},{7,9},{8... | collective-permute-start | bytes 331784 | tf_op jit(solution)/shard_map/ppermute | solution.py:502
  23.5 0.0 copy-done.1
  23.5 6.8 %collective-permute-start.2 = (f32[216,128]{1,0:T(8,128)S(1)}, f32[216,128]{1,0:T(8,128)}, u32[]{:S(2)}, u32[]{:S(2)}) collective-permute-start(f32[216,128]{1,0:T(8,128)S(1)} %copy-done.1), channel_id=1, source_target_pairs={{1,0},{2,1},{3,2},{4,3},{5,4},{6,5},{7,6},{8,7},{9,8},{10,9},{11,1... | collective-permute-start | bytes 331784 | tf_op jit(solution)/shard_map/ppermute | solution.py:502
  30.3 0.0 copy-done
  30.3 1.1 %collective-permute-start.3 = (f32[216,128]{1,0:T(8,128)S(1)}, f32[216,128]{1,0:T(8,128)}, u32[]{:S(2)}, u32[]{:S(2)}) collective-permute-start(f32[216,128]{1,0:T(8,128)S(1)} %copy-done), channel_id=1, source_target_pairs={{2,0},{3,1},{4,2},{5,3},{6,4},{7,5},{8,6},{9,7},{10,8},{11,9},{12,... | collective-permute-start | bytes 331784 | tf_op jit(solution)/shard_map/ppermute | solution.py:502
  31.4 1.9 %collective-permute-done.refs_14_ = f32[216,128]{1,0:T(8,128)} collective-permute-done((f32[216,128]{1,0:T(8,128)}, f32[216,128]{1,0:T(8,128)}, u32[]{:S(2)}, u32[]{:S(2)}) %collective-permute-start) | collective-permute-done | bytes 110624 | tf_op jit(solution)/shard_map/ppermute | solution.py:502
  33.3 0.9 %collective-permute-done.1.refs_15_ = f32[216,128]{1,0:T(8,128)} collective-permute-done((f32[216,128]{1,0:T(8,128)}, f32[216,128]{1,0:T(8,128)}, u32[]{:S(2)}, u32[]{:S(2)}) %collective-permute-start.1) | collective-permute-done | bytes 110624 | tf_op jit(solution)/shard_map/ppermute | solution.py:502
  34.2 0.0 collective-permute-done.2.refs_16_
  34.2 1.0 %collective-permute-done.3.refs_17_ = f32[216,128]{1,0:T(8,128)} collective-permute-done((f32[216,128]{1,0:T(8,128)S(1)}, f32[216,128]{1,0:T(8,128)}, u32[]{:S(2)}, u32[]{:S(2)}) %collective-permute-start.3) | collective-permute-done | bytes 110624 | tf_op jit(solution)/shard_map/ppermute | solution.py:502
  35.2 9.9 %shard_map.137 = (f32[9,56,256]{2,1,0:T(8,128)}, f32[216,256]{1,0:T(8,128)}, bf16[56,288]{1,0:T(8,128)(2,1)}, bf16[2,72,24]{2,1,0:T(8,128)(2,1)}) custom-call(f32[3,56,56]{2,1,0:T(8,128)} %refs_0_.4, f32[21,4,56]{2,1,0:T(4,128)} %bitcast.10, bf16[128,1152]{1,0:T(8,128)(2,1)} %get-tuple-element.20.refs_2_, bf16[128,1152]{1,0:T(8,128)(2,1)} %get-tuple-element.21.refs_3_, ...), custom_call_target="tpu_custom_call" | custom-call | flops 100000000 | bytes 3000000 | tf_op jit(solution)/shard_map/pallas_call | solution.py:516
  45.1 0.0 all-to-all-done.refs_1_
  45.1 3.8 %shard_map.138 = f32[9,56,256]{2,1,0:T(8,128)} custom-call(s32[3,128]{1,0:T(4,128)} %refs_0_.5, f32[128,2,128]{2,1,0:T(2,128)} %all-to-all-done.refs_1_, bf16[2,72,24]{2,1,0:T(8,128)(2,1)} %get-tuple-element.29.refs_2_, f32[216,256]{1,0:T(8,128)} %get-tuple-element.30.refs_3_, bf16[56,288]{1,0:T(8,128)(2,1)} %get-tuple-element.31.refs_4_, ...), custom_call_target="tpu_custom_call" | custom-call | flops 100000000 | bytes 3000000 | tf_op jit(solution)/shard_map/pallas_call | solution.py:516
Async XLA Ops:
  10.6 12.9 %copy-start.1 = (f32[216,128]{1,0:T(8,128)S(1)}, f32[216,128]{1,0:T(8,128)}, u32[]{:S(2)}) copy-start(f32[216,128]{1,0:T(8,128)} %get-tuple-element.27) | copy-start | bytes 331780
  10.6 19.7 %copy-start = (f32[216,128]{1,0:T(8,128)S(1)}, f32[216,128]{1,0:T(8,128)}, u32[]{:S(2)}) copy-start(f32[216,128]{1,0:T(8,128)} %get-tuple-element.28) | copy-start | bytes 331780
  10.6 34.5 %all-to-all-start = ((f32[128,2,128]{2,1,0:T(2,128)}), f32[128,2,128]{2,1,0:T(2,128)}, u32[]{:S(2)}, u32[]{:S(2)}) async-start(f32[128,2,128]{2,1,0:T(2,128)} %get-tuple-element.19), calls=%async_computation | async-start | bytes 262144 | tf_op jit(solution)/shard_map/all_to_all | solution.py:554
  22.3 11.0 %collective-permute-start = (f32[216,128]{1,0:T(8,128)}, f32[216,128]{1,0:T(8,128)}, u32[]{:S(2)}, u32[]{:S(2)}) collective-permute-start(f32[216,128]{1,0:T(8,128)} %get-tuple-element.25), channel_id=1, source_target_pairs={{127,0},{0,1},{1,2},{2,3},{3,4},{4,5},{5,6},{6,7},{7,8},{8,9},{9,1... | collective-permute-start | bytes 331784 | tf_op jit(solution)/shard_map/ppermute | solution.py:502
  22.4 11.8 %collective-permute-start.1 = (f32[216,128]{1,0:T(8,128)}, f32[216,128]{1,0:T(8,128)}, u32[]{:S(2)}, u32[]{:S(2)}) collective-permute-start(f32[216,128]{1,0:T(8,128)} %get-tuple-element.26), channel_id=1, source_target_pairs={{126,0},{127,1},{0,2},{1,3},{2,4},{3,5},{4,6},{5,7},{6,8},{7,9},{8... | collective-permute-start | bytes 331784 | tf_op jit(solution)/shard_map/ppermute | solution.py:502
  23.5 10.6 %collective-permute-start.2 = (f32[216,128]{1,0:T(8,128)S(1)}, f32[216,128]{1,0:T(8,128)}, u32[]{:S(2)}, u32[]{:S(2)}) collective-permute-start(f32[216,128]{1,0:T(8,128)S(1)} %copy-done.1), channel_id=1, source_target_pairs={{1,0},{2,1},{3,2},{4,3},{5,4},{6,5},{7,6},{8,7},{9,8},{10,9},{11,1... | collective-permute-start | bytes 331784 | tf_op jit(solution)/shard_map/ppermute | solution.py:502
  30.3 4.9 %collective-permute-start.3 = (f32[216,128]{1,0:T(8,128)S(1)}, f32[216,128]{1,0:T(8,128)}, u32[]{:S(2)}, u32[]{:S(2)}) collective-permute-start(f32[216,128]{1,0:T(8,128)S(1)} %copy-done), channel_id=1, source_target_pairs={{2,0},{3,1},{4,2},{5,3},{6,4},{7,5},{8,6},{9,7},{10,8},{11,9},{12,... | collective-permute-start | bytes 331784 | tf_op jit(solution)/shard_map/ppermute | solution.py:502
